TPU v7x, 256 devices: a whole 4x4x8 slice. The times are simulated.
256 devices in a mesh: tensor: 64 (over z_lo, x, y, core), dp: 4 (over z_hi).
Axes of the slice: x: 4, y: 4, z: 8 (z_hi: 4, z_lo: 2; z = z_hi * 2 + z_lo), core: 2. Of those that a mesh axis runs over, the one named last changes fastest.
Arguments:
- cotangent: bfloat16 [1024, 8192], P('dp', 'tensor'), may hold values from -12 to 12
- down_weight: bfloat16 [28672, 8192], P('tensor', 'dp'), may hold values from -0.0625 to 0.0625
- gate_pre: bfloat16 [1024, 28672], P('dp', 'tensor'), may hold values from -6 to 6
- up_pre: bfloat16 [1024, 28672], P('dp', 'tensor'), may hold values from -6 to 6
Outputs:
- factor: bfloat16 [64, 2, 33, 4, 50176], P('tensor', None, None, 'dp')
All inputs are finite; a program needn't handle non-finite values.
Results may differ from a plain program's by a relative error of at most 0.0057.
Values may be sent and summed in bfloat16 or wider, within the bound.
A program may use at most 128 MiB of HBM per device.

v0:
```python
import jax
import jax.numpy as jnp
from jax import lax
from jax.sharding import PartitionSpec as P


def per_device(cotangent, down_weight, gate_pre, up_pre):
    block_count = lax.axis_size("tensor")
    groups = lax.axis_size("dp")
    own_block = lax.axis_index("tensor")
    group_index = lax.axis_index("dp")
    local_tokens = gate_pre.shape[0]
    block_width = gate_pre.shape[1]
    slice_width = block_width // groups
    all_tokens = local_tokens * groups
    band_width = block_count // 2 + 1
    contract = (((1,), (1,)), ((), ()))
    features = lax.all_gather(cotangent, "tensor", axis=1, tiled=True)
    hidden_cot = lax.dot_general(
        features,
        lax.all_gather(down_weight, "dp", axis=1, tiled=True),
        contract,
        preferred_element_type=jnp.float32,
    )
    gate_value = gate_pre.astype(jnp.float32)
    up_value = up_pre.astype(jnp.float32)
    sigmoid_gate = jax.nn.sigmoid(gate_value)
    grad_gate = (
        hidden_cot * up_value * sigmoid_gate * (1.0 + gate_value * (1.0 - sigmoid_gate))
    ).astype(jnp.bfloat16)
    grad_up = (hidden_cot * gate_value * sigmoid_gate).astype(jnp.bfloat16)
    stacked = jnp.stack([grad_gate, grad_up])
    own_rows = lax.all_gather(stacked, "dp", axis=1, tiled=True)
    own_slice = lax.dynamic_slice_in_dim(own_rows, group_index * slice_width, slice_width, 2)
    inverse_count = 1.0 / all_tokens

    def factor_tile(partner):
        product = jnp.einsum("ftr,ftc->frc", own_rows, partner, preferred_element_type=jnp.float32)
        return (product * inverse_count).astype(jnp.bfloat16)

    def place(result, offset, partner):
        return lax.dynamic_update_slice(
            result,
            factor_tile(partner)[:, None],
            (jnp.int32(0), offset, jnp.int32(0), jnp.int32(0)),
        )

    holder = jnp.zeros((2, band_width, block_width, slice_width), jnp.bfloat16)
    block_piece = lax.all_gather(own_slice[None], "tensor", axis=0, tiled=True)

    def place_block(position, current):
        offset = (own_block - position) % block_count
        partner = lax.dynamic_index_in_dim(block_piece, position, 0, keepdims=False)
        return lax.cond(
            offset < band_width,
            lambda kept: place(kept, offset, partner),
            lambda kept: kept,
            current,
        )

    factor = lax.fori_loop(0, block_piece.shape[0], place_block, holder)
    flat = factor.reshape(2, band_width, block_width * slice_width)
    return flat[None, :, :, None, :]


def solution(mesh):
    placed = (P("dp", "tensor"), P("tensor", "dp"), P("dp", "tensor"), P("dp", "tensor"))
    return jax.shard_map(
        per_device,
        mesh=mesh,
        in_specs=placed,
        out_specs=P("tensor", None, None, "dp", None),
        check_vma=False,
    )
```

profile of v0, /device:TPU:1, one launch (start us, length us, event | category | flops | bytes accessed | tf_op | source)
XLA Modules:
  0.0 617.8 jit_solution(3863569441559747056)
XLA Ops:
  8.1 121.4 %all-gather.6.cloned.1.call-done = bf16[256,8192]{1,0:T(8,128)(2,1)} async-done(((bf16[256,128]{1,0:T(8,128)(2,1)}), bf16[256,8192]{1,0:T(8,128)(2,1)}) %all-gather.6.cloned.1.call-update) | async-done | bytes 4194320 | tf_op jit(solution)/shard_map/all_gather | solution.py:18
  129.5 137.8 %all-gather.8.cloned.1.call-done = bf16[448,8192]{1,0:T(8,128)(2,1)} async-done(((bf16[448,2048]{1,0:T(8,128)(2,1)}), bf16[448,8192]{1,0:T(8,128)(2,1)}) %all-gather.8.cloned.1.call-update) | async-done | bytes 7340048 | tf_op jit(solution)/shard_map/all_gather | solution.py:21
  267.3 6.5 %fusion.15 = (bf16[1,256,448]{1,2,0:T(8,128)(2,1)S(1)}, bf16[1,256,448]{1,2,0:T(8,128)(2,1)S(1)}) fusion(bf16[256,448]{0,1:T(8,128)(2,1)} %param.10, bf16[256,448]{0,1:T(8,128)(2,1)} %param.11, bf16[256,8192]{1,0:T(8,128)(2,1)} %all-gather.6.cloned.1.call-done, bf16[448,8192]{1,0:T(8,128)(2,1)} %all-gather.8.cloned.1.call-done), kind=kOutput, calls=%fused_computation.20 | convolution fusion | flops 1880768512 | bytes 12451840 | tf_op jit(solution)/shard_map/dot_general | solution.py:19
  274.7 50.5 %all-gather.10.cloned.1.call-done = bf16[2,1024,448]{1,2,0:T(8,128)(2,1)} async-done(((bf16[2,256,448]{1,2,0:T(8,128)(2,1)}), bf16[2,1024,448]{1,2,0:T(8,128)(2,1)}) %all-gather.10.cloned.1.call-update) | async-done | bytes 1835024 | tf_op jit(solution)/shard_map/all_gather | solution.py:33
  327.2 167.3 %all-gather.12.cloned.1.call-done = bf16[128,1024,112]{1,2,0:T(8,128)(2,1)} async-done(((bf16[2,1024,112]{1,2,0:T(8,128)(2,1)}), bf16[128,1024,112]{1,2,0:T(8,128)(2,1)}) %all-gather.12.cloned.1.call-update) | async-done | bytes 29360144 | tf_op jit(solution)/shard_map/all_gather | solution.py:49
  494.4 3.9 broadcast_in_dim.10
  498.4 80.2 %while.18 = (s32[]{:T(128)}, bf16[2,33,448,112]{2,3,0,1:T(8,128)(2,1)}, s32[]{:T(128)}, bf16[64,2,1024,112]{2,3,1,0:T(8,128)(2,1)}, bf16[2,1024,448]{1,2,0:T(8,1...) while((s32[]{:T(128)}, bf16[2,33,448,112]{2,3,0,1:T(8,128)(2,1)}, s32[]{:T(128)}, ...), condition=%wide.region_3.4_spmd, body=%wide.region_0.3_spmd.sunk | while | flops 205721616 | bytes 2523496 | solution.py:61
  498.4 2.4 conditional.2
  498.4 2.4 fusion.2
  500.8 2.4 conditional.2
  500.8 2.4 fusion.2
  504.5 2.4 conditional.2
  504.6 2.4 fusion.2
  514.1 2.4 conditional.2
  514.1 2.4 fusion.2
  516.5 2.4 conditional.2
  516.5 2.4 fusion.2
  521.3 2.4 conditional.2
  521.3 2.4 fusion.2
  526.1 2.4 conditional.2
  526.1 2.4 fusion.2
  528.5 2.4 conditional.2
  528.5 2.4 fusion.2
  530.9 2.4 conditional.2
  533.2 2.4 conditional.2
  533.2 2.4 fusion.2
  542.8 2.4 conditional.2
  542.8 2.4 fusion.2
  552.3 2.4 conditional.2
  552.3 2.4 fusion.2
  554.7 2.4 conditional.2
  554.7 2.4 fusion.2
  557.1 2.4 conditional.2
  557.1 2.4 fusion.2
  559.5 2.4 conditional.2
  559.5 2.4 fusion.2
  561.9 2.4 conditional.2
  561.9 2.4 fusion.2
  564.3 2.4 conditional.2
  564.3 2.4 fusion.2
  566.7 2.4 conditional.2
  566.7 2.4 fusion.2
  573.8 2.4 conditional.2
  573.8 2.4 fusion.2
  576.2 2.4 conditional.2
  576.2 2.4 fusion.2
  578.6 10.8 %copy.6 = bf16[2,33,448,112]{3,2,0,1:T(8,128)(2,1)} copy(bf16[2,33,448,112]{2,3,0,1:T(8,128)(2,1)} %get-tuple-element.191) | data formatting | bytes 13246464 | tf_op jit(solution)/shard_map/while | solution.py:61
  589.5 21.8 %broadcast_in_dim_reshape.3 = bf16[1,2,33,1,50176]{4,1,3,2,0:T(2,128)(2,1)} reshape(bf16[2,33,448,112]{3,2,0,1:T(8,128)(2,1)} %copy.6) | data formatting | bytes 13246464 | tf_op jit(solution)/shard_map/broadcast_in_dim;reshape | solution.py:63
  (70 shorter events, 68.9 us)
Async XLA Ops:
  6.5 122.9 %all-gather.6.cloned.1.call-start = ((), (), s32[]{:S(2)}) async-start(), calls=%async_computation | async-start | bytes 4259840 | tf_op jit(solution)/shard_map/all_gather | solution.py:18
  7.3 260.0 %all-gather.8.cloned.1.call-start = ((), (), s32[]{:S(2)}) async-start(), calls=%async_computation.1 | async-start | bytes 9175040 | tf_op jit(solution)/shard_map/all_gather | solution.py:21
  8.0 317.2 %all-gather.10.cloned.1.call-start = ((), (), s32[]{:S(2)}) async-start(), calls=%async_computation.2 | async-start | bytes 2293760 | tf_op jit(solution)/shard_map/all_gather | solution.py:33
  274.7 219.8 %all-gather.12.cloned.1.call-start = ((), (), s32[]{:S(2)}) async-start(), calls=%async_computation.3 | async-start | bytes 29818880 | tf_op jit(solution)/shard_map/all_gather | solution.py:49
  325.2 173.2 %copy-start = (bf16[2,1024,448]{1,2,0:T(8,128)(2,1)S(1)}, bf16[2,1024,448]{1,2,0:T(8,128)(2,1)}, u32[]{:S(2)}) copy-start(bf16[2,1024,448]{1,2,0:T(8,128)(2,1)} %all-gather.10.cloned.1.call-done) | copy-start | bytes 5505028
Sparse Core Ops, SparseCore 0:
  9.1 120.3 all-gather.5
  131.3 135.9 all-gather.7
  274.8 50.3 all-gather.9
  327.3 167.1 all-gather.11
where the time goes:
time: 620 us; the launch traced here: 618 us
  waiting for transfers between devices  478 us (77%)
  matrix products  85.4 us (14%)
  local copies, waits for them, and re-layouts  38.5 us (6%)
  between operations  13.1 us (2%)
    all_gather x1, waiting for transfers between devices, per_device(): block_piece = lax.all_gather(own_slice[None], 'tensor', axis=0, tiled=True)  167 us
    all_gather x1, waiting for transfers between devices, per_device(): lax.all_gather(down_weight, 'dp', axis=1, tiled=True)  138 us
    all_gather x1, waiting for transfers between devices, per_device(): features = lax.all_gather(cotangent, 'tensor', axis=1, tiled=True)  121 us
    dot_general x33, matrix products, factor_tile(): jnp.einsum('ftr,ftc->frc', own_rows, partner, preferred_element_type=jnp....  78.8 us
    all_gather x1, waiting for transfers between devices, per_device(): own_rows = lax.all_gather(stacked, 'dp', axis=1, tiled=True)  50.5 us
    another operation x1, local copies, waits for them, and re-layouts, per_device(): return flat[None, :, :, None, :]  21.8 us
  transfers between devices with their start and end apart: 4, of which 4 were waited for; matrix products, arithmetic and copies ran while one was open for 0% of the time, Pallas kernels for 0%

commit v1 on v0

--- a/solution.py
+++ b/solution.py
@@ -2,6 +2,11 @@
 import jax.numpy as jnp
 from jax import lax
 from jax.sharding import PartitionSpec as P
+
+
+def all_by_exchange(x, axis, d):
+    repeated = jnp.stack([x] * lax.axis_size(axis))
+    return jnp.concatenate(lax.all_to_all(repeated, axis, 0, 0), axis=d)
 
 
 def per_device(cotangent, down_weight, gate_pre, up_pre):
@@ -46,7 +51,7 @@
         )
 
     holder = jnp.zeros((2, band_width, block_width, slice_width), jnp.bfloat16)
-    block_piece = lax.all_gather(own_slice[None], "tensor", axis=0, tiled=True)
+    block_piece = all_by_exchange(own_slice[None], "tensor", 0)
 
     def place_block(position, current):
         offset = (own_block - position) % block_count

time: 620 us -> 906 us (1.46); the launches traced: 618 us -> 893 us
  waiting for transfers between devices: 478 us -> 738 us
    all_to_all x0 -> x1, waiting for transfers between devices: none -> 427 us  [all_by_exchange(): return jnp.concatenate(lax.all_to_all(repeated, axis, 0, 0), axis=d)]
    all_gather x1 -> x0, waiting for transfers between devices: 167 us -> none  [per_device(): block_piece = lax.all_gather(own_slice[None], 'tensor', axis=0, tiled=True)]
    another operation x0 -> x1, local copies, waits for them, and re-layouts: none -> 9.88 us  [all_by_exchange(): repeated = jnp.stack([x] * lax.axis_size(axis))]
where the time goes in v1:
time: 906 us; the launch traced here: 893 us
  waiting for transfers between devices  738 us (81%)
  matrix products  85.2 us (9%)
  local copies, waits for them, and re-layouts  47.5 us (5%)
  between operations  13.1 us (1%)
    all_to_all x1, waiting for transfers between devices, all_by_exchange(): return jnp.concatenate(lax.all_to_all(repeated, axis, 0, 0), axis=d)  427 us
    all_gather x1, waiting for transfers between devices, per_device(): lax.all_gather(down_weight, 'dp', axis=1, tiled=True)  138 us
    all_gather x1, waiting for transfers between devices, per_device(): features = lax.all_gather(cotangent, 'tensor', axis=1, tiled=True)  121 us
    dot_general x33, matrix products, factor_tile(): jnp.einsum('ftr,ftc->frc', own_rows, partner, preferred_element_type=jnp....  78.7 us
    all_gather x1, waiting for transfers between devices, per_device(): own_rows = lax.all_gather(stacked, 'dp', axis=1, tiled=True)  50.5 us
    another operation x1, local copies, waits for them, and re-layouts, per_device(): return flat[None, :, :, None, :]  21.8 us
  transfers between devices with their start and end apart: 4, of which 4 were waited for; matrix products, arithmetic and copies ran while one was open for 0% of the time, Pallas kernels for 0%

profile of v1, /device:TPU:1, one launch (start us, length us, event | category | flops | bytes accessed | tf_op | source)
XLA Modules:
  0.0 893.3 jit_solution(12596353697504210007)
XLA Ops:
  8.1 121.4 %all-gather.4.cloned.1.call-done = bf16[256,8192]{1,0:T(8,128)(2,1)} async-done(((bf16[256,128]{1,0:T(8,128)(2,1)}), bf16[256,8192]{1,0:T(8,128)(2,1)}) %all-gather.4.cloned.1.call-update) | async-done | bytes 4194320 | tf_op jit(solution)/shard_map/all_gather | solution.py:23
  129.5 137.8 %all-gather.6.cloned.1.call-done = bf16[448,8192]{1,0:T(8,128)(2,1)} async-done(((bf16[448,2048]{1,0:T(8,128)(2,1)}), bf16[448,8192]{1,0:T(8,128)(2,1)}) %all-gather.6.cloned.1.call-update) | async-done | bytes 7340048 | tf_op jit(solution)/shard_map/all_gather | solution.py:26
  267.3 6.5 fusion.15
  274.6 50.5 %all-gather.8.cloned.1.call-done = bf16[2,1024,448]{1,2,0:T(8,128)(2,1)} async-done(((bf16[2,256,448]{1,2,0:T(8,128)(2,1)}), bf16[2,1024,448]{1,2,0:T(8,128)(2,1)}) %all-gather.8.cloned.1.call-update) | async-done | bytes 1835024 | tf_op jit(solution)/shard_map/all_gather | solution.py:38
  326.2 9.9 %stack.15 = bf16[64,1,2,1024,112]{3,4,2,1,0:T(8,128)(2,1)} broadcast(bf16[2,1024,112]{1,2,0:T(8,128)(2,1)S(1)} %constant_dynamic-slice_fusion), dimensions={2,3,4} | broadcast | bytes 29818880 | tf_op jit(solution)/shard_map/stack | solution.py:8
  336.1 7.1 all-to-all-start
  343.2 426.9 %all-to-all-done = bf16[64,1,2,1024,112]{3,4,2,1,0:T(8,128)(2,1)} async-done(((bf16[64,1,2,1024,112]{3,4,2,1,0:T(8,128)(2,1)}), bf16[64,1,2,1024,112]{3,4,2,1,0:T(8,128)(2,1)}, u32[]{:S(2)}, u32[]{:S(2)}) %all-to-all-start) | async-done | bytes 29360160 | tf_op jit(solution)/shard_map/all_to_all | solution.py:9
  770.1 3.9 broadcast_in_dim.7
  774.0 80.1 %while.18 = (s32[]{:T(128)}, bf16[2,33,448,112]{2,3,0,1:T(8,128)(2,1)}, s32[]{:T(128)}, bf16[64,2,1024,112]{2,3,1,0:T(8,128)(2,1)}, bf16[2,1024,448]{1,2,0:T(8,1...) while((s32[]{:T(128)}, bf16[2,33,448,112]{2,3,0,1:T(8,128)(2,1)}, s32[]{:T(128)}, ...), condition=%wide.region_3.4_spmd, body=%wide.region_0.3_spmd.sunk | while | flops 205721616 | bytes 2523496 | solution.py:66
  774.0 2.4 conditional.2
  774.0 2.4 fusion.2
  776.5 2.4 conditional.2
  776.5 2.4 fusion.2
  780.2 2.4 conditional.2
  780.2 2.4 fusion.2
  785.0 2.4 conditional.2
  785.0 2.4 fusion.2
  787.4 2.4 conditional.2
  787.4 2.4 fusion.2
  789.8 2.4 conditional.2
  789.8 2.4 fusion.2
  792.1 2.4 conditional.2
  792.1 2.4 fusion.2
  801.7 2.4 conditional.2
  801.7 2.4 fusion.2
  808.8 2.4 conditional.2
  808.8 2.4 fusion.2
  813.6 2.4 conditional.2
  816.0 2.4 conditional.2
  820.7 2.4 conditional.2
  823.1 2.4 conditional.2
  823.1 2.4 fusion.2
  827.9 2.4 conditional.2
  827.9 2.4 fusion.2
  830.3 2.4 conditional.2
  832.7 2.4 conditional.2
  832.7 2.4 fusion.2
  835.1 2.4 conditional.2
  837.5 2.4 conditional.2
  837.5 2.4 fusion.2
  839.8 2.4 conditional.2
  839.9 2.4 fusion.2
  849.4 2.4 conditional.2
  849.4 2.4 fusion.2
  851.8 2.4 conditional.2
  851.8 2.4 fusion.2
  854.2 10.8 %copy.6 = bf16[2,33,448,112]{3,2,0,1:T(8,128)(2,1)} copy(bf16[2,33,448,112]{2,3,0,1:T(8,128)(2,1)} %get-tuple-element.191) | data formatting | bytes 13246464 | tf_op jit(solution)/shard_map/while | solution.py:66
  865.0 21.8 %broadcast_in_dim_reshape.3 = bf16[1,2,33,1,50176]{4,1,3,2,0:T(2,128)(2,1)} reshape(bf16[2,33,448,112]{3,2,0,1:T(8,128)(2,1)} %copy.6) | data formatting | bytes 13246464 | tf_op jit(solution)/shard_map/broadcast_in_dim;reshape | solution.py:68
  (70 shorter events, 72.6 us)
Async XLA Ops:
  6.5 122.9 %all-gather.4.cloned.1.call-start = ((), (), s32[]{:S(2)}) async-start(), calls=%async_computation.1 | async-start | bytes 4259840 | tf_op jit(solution)/shard_map/all_gather | solution.py:23
  7.3 260.0 %all-gather.6.cloned.1.call-start = ((), (), s32[]{:S(2)}) async-start(), calls=%async_computation.2 | async-start | bytes 9175040 | tf_op jit(solution)/shard_map/all_gather | solution.py:26
  8.0 317.1 %all-gather.8.cloned.1.call-start = ((), (), s32[]{:S(2)}) async-start(), calls=%async_computation.3 | async-start | bytes 2293760 | tf_op jit(solution)/shard_map/all_gather | solution.py:38
  336.1 434.0 %all-to-all-start = ((bf16[64,1,2,1024,112]{3,4,2,1,0:T(8,128)(2,1)}), bf16[64,1,2,1024,112]{3,4,2,1,0:T(8,128)(2,1)}, u32[]{:S(2)}, u32[]{:S(2)}) async-start(bf16[64,1,2,1024,112]{3,4,2,1,0:T(8,128)(2,1)} %stack.15), calls=%async_computation | async-start | bytes 58720256 | tf_op jit(solution)/shard_map/all_to_all | solution.py:9
  343.2 430.8 %copy-start = (bf16[2,1024,448]{1,2,0:T(8,128)(2,1)S(1)}, bf16[2,1024,448]{1,2,0:T(8,128)(2,1)}, u32[]{:S(2)}) copy-start(bf16[2,1024,448]{1,2,0:T(8,128)(2,1)} %all-gather.8.cloned.1.call-done) | copy-start | bytes 5505028
Sparse Core Ops, SparseCore 0:
  9.1 120.3 all-gather.3
  131.3 135.9 all-gather.5
  274.7 50.3 all-gather.7
